TPU v7x, 32 devices: a whole 2x2x4 slice. The times are simulated.
32 devices in a mesh: rad: 8 (over z, y), mode: 4 (over x, core).
Axes of the slice: x: 2, y: 2, z: 4, core: 2. Of those that a mesh axis runs over, the one named last changes fastest.
Arguments:
- coefficients: bfloat16 [3, 2, 256, 8, 4, 1152], P(None, None, 'rad', None, 'mode'), may hold values from -6 to 6
- legendre: bfloat16 [8, 4, 1152, 2048], P('rad', 'mode'), may hold values from -0.25 to 0.25
- radial_left_factor: float32 [3, 256, 256], replicated, may hold values from -0.375 to 0.375
- radial_right: float32 [3, 256, 256], replicated, may hold values from -0.375 to 0.375
- eigen_rates: float32 [3, 256], replicated, may hold values from 0.02 to 4
- diffusivity: float32 [3], replicated, may hold values from 0.5 to 4
- slot_order: int32 [8, 4, 2], P('rad', 'mode'), may hold values from 0 to 1023, as said below
- slot_start: int32 [8, 4, 2], P('rad', 'mode'), may hold values from 0 to 1024, as said below
Outputs:
- physical: bfloat16 [3, 2, 8, 4, 256, 2, 2048], P(None, None, None, None, 'rad', None, 'mode')
Inputs may be any that keep to these rules, and one draw needn't show every extreme that they name: `slot_order`: the 64 orders are distinct, 0 and 1023 among them; the two rows of every group have block counts 1024 / 128 - floor(m / 128) that add up to exactly 9. `slot_start`: in every group the first row starts at slot 0 and the second at 128 times the first row's block count.
All inputs are finite; a program needn't handle non-finite values.
Results may differ from a plain program's by a relative error of at most 0.0049.
Values may be sent and summed in bfloat16 or wider, within the bound.
A program may use at most 256 MiB of HBM per device.

v0:
```python
import functools
import jax
import jax.numpy as jnp
from jax import lax
from jax.experimental import pallas as pl
from jax.experimental.pallas import tpu as pltpu
from jax.sharding import PartitionSpec as P

DEGREES = 1024
BLOCK = 128
MESH = pl.DeviceIdType.MESH


def far_first(count):
    return sorted(range(count), key=lambda k: (-min(k, count - k), k))


def whole_kernel(
    rads,
    modes,
    parts_count,
    order_ref,
    start_ref,
    diffusivity_ref,
    eigen_ref,
    left_hbm,
    right_hbm,
    x_ref,
    legendre_ref,
    o_ref,
    left_ref,
    right_ref,
    entering,
    outgoing,
    arrived,
    polynomial_rows,
    updated,
    held,
    enter_sem,
    in_send,
    in_recv,
    factor_sem,
    legendre_sem,
    out_send,
    out_recv,
    out_local,
):
    my_rad = lax.axis_index("rad")
    my_mode = lax.axis_index("mode")
    devices = rads * modes
    parts = arrived.shape[0]
    packed = arrived.shape[3]
    radii = right_ref.shape[1]
    rows, lats = held.shape[1], held.shape[3]
    me = my_rad * modes + my_mode

    def enter(c):
        return pltpu.make_async_copy(x_ref.at[c], entering.at[c], enter_sem.at[c])

    for c in range(parts):
        enter(c).start()
    fetches = (
        pltpu.make_async_copy(left_hbm, left_ref, factor_sem.at[0]),
        pltpu.make_async_copy(right_hbm, right_ref, factor_sem.at[1]),
        pltpu.make_async_copy(legendre_ref, polynomial_rows, legendre_sem),
    )
    for fetch in fetches:
        fetch.start()
    barrier = pltpu.get_barrier_semaphore()
    for ka in range(rads):
        for kb in range(modes):
            if ka or kb:
                peer = (lax.rem(my_rad + ka, rads), lax.rem(my_mode + kb, modes))
                pl.semaphore_signal(barrier, inc=1, device_id=peer, device_id_type=MESH)

    def turn(c):
        enter(c).wait()
        outgoing[c] = jnp.swapaxes(entering[c], 0, 1)

    turn(0)
    pl.semaphore_wait(barrier, devices - 1)

    def send_part(c, carry):
        @pl.when(c > 0)
        def _():
            turn(c)

        for ka in far_first(rads):
            a = lax.rem(my_rad + ka, rads)
            source = outgoing.at[c, a]
            target = arrived.at[c, my_rad]
            if ka:
                pltpu.make_async_remote_copy(
                    src_ref=source,
                    dst_ref=target,
                    send_sem=in_send,
                    recv_sem=in_recv.at[c],
                    device_id=(a, my_mode),
                    device_id_type=MESH,
                ).start()
            else:
                pltpu.make_async_copy(source, target, in_recv.at[c]).start()
        return carry

    lax.fori_loop(0, parts, send_part, 0)

    position = lax.broadcasted_iota(jnp.int32, (1, packed), 1)
    live = []
    degree = jnp.zeros((1, packed), jnp.int32)
    for s in range(2):
        order = order_ref[0, 0, s]
        start = start_ref[0, 0, s]
        first_degree = BLOCK * (order // BLOCK)
        inside = (position >= start) & (position < start + DEGREES - first_degree)
        row_degree = first_degree + position - start
        degree = degree + jnp.where(inside, row_degree, 0)
        live.append(jnp.where(inside & (row_degree >= order), 1.0, 0.0).astype(jnp.float32))
    degree_level = degree.astype(jnp.float32)
    harmonic = degree_level * (degree_level + 1.0) / (DEGREES * DEGREES)
    covered = jnp.maximum(live[0], live[1])
    row = lax.broadcasted_iota(jnp.int32, (2 * radii, radii), 0)
    column = lax.broadcasted_iota(jnp.int32, (2 * radii, radii), 1)
    doubling = jnp.where(row // 2 == column, 1.0, 0.0).astype(jnp.bfloat16)
    parity = lax.broadcasted_iota(jnp.int32, (2 * radii, packed), 0) % 2
    for fetch in fetches:
        fetch.wait()

    def one_part(c, carry):
        field = c // parts_count
        pltpu.make_async_copy(arrived.at[c], arrived.at[c], in_recv.at[c]).wait()
        rates = eigen_ref[pl.ds(field, 1), :]
        rates = jnp.transpose(jnp.broadcast_to(rates, (128, radii)))[:, 0:1]
        shrink = 1.0 + rates + diffusivity_ref[field] * harmonic
        values = arrived[c].reshape(radii, packed).astype(jnp.float32)
        turned = jnp.dot(
            left_ref[field], values, precision=lax.Precision.HIGHEST, preferred_element_type=jnp.float32
        )
        scaled = turned * (covered / shrink)
        result = jnp.dot(
            right_ref[field], scaled, precision=lax.Precision.HIGHEST, preferred_element_type=jnp.float32
        )
        doubled = jnp.dot(doubling, result.astype(jnp.bfloat16), preferred_element_type=jnp.float32)
        updated[...] = (doubled * jnp.where(parity == 0, live[0], live[1])).astype(jnp.bfloat16)
        for kb in range(modes):
            b = lax.rem(my_mode + kb, modes)
            columns = pl.ds(pl.multiple_of(b * lats, lats), lats)
            summed = jnp.dot(
                updated[...], polynomial_rows[:, columns], preferred_element_type=jnp.float32
            )
            blocks = summed.reshape(rads, rows, 2, lats).astype(jnp.bfloat16)
            for a in range(rads):
                held[(c * modes + kb) * rads + a] = blocks[a]
            for ka in far_first(rads):
                a = lax.rem(my_rad + ka, rads)
                source = held.at[(c * modes + kb) * rads + a]
                target = o_ref.at[c * devices + me]
                if ka or kb:
                    pltpu.make_async_remote_copy(
                        src_ref=source,
                        dst_ref=target,
                        send_sem=out_send,
                        recv_sem=out_recv,
                        device_id=(a, b),
                        device_id_type=MESH,
                    ).start()
                else:
                    pltpu.make_async_copy(source, target, out_local).start()
        return carry

    lax.fori_loop(0, parts, one_part, 0)
    others = arrived.at[:, pl.ds(0, rads - 1)]
    pltpu.make_async_copy(others, others, in_send).wait()
    remote = pl.ds(0, parts * (devices - 1))
    pltpu.make_async_copy(held.at[remote], held.at[remote], out_send).wait()
    pltpu.make_async_copy(o_ref.at[remote], o_ref.at[remote], out_recv).wait()
    own = pl.ds(0, parts)
    pltpu.make_async_copy(held.at[own], o_ref.at[own], out_local).wait()


PLANES = 4
EARLY = 2
SHORT_AFTER = 2
PIECES = 4
UNIT = 16


def pieces_of(value, count):
    pieces = []
    for _ in range(count):
        piece = value.astype(jnp.bfloat16)
        pieces.append(piece)
        value = value - piece.astype(jnp.float32)
    return pieces


def product(left, right):
    return jnp.dot(left, right, preferred_element_type=jnp.float32)


def factored_kernel(
    rads,
    modes,
    parts_count,
    unit_room,
    block_room,
    order_ref,
    start_ref,
    diffusivity_ref,
    eigen_ref,
    left_hbm,
    right_hbm,
    x_ref,
    legendre_ref,
    o_ref,
    flag_ref,
    left_ref,
    right_ref,
    entering,
    outgoing,
    arrived,
    polynomial_rows,
    updated,
    updated_far,
    held,
    long_out,
    long_in,
    short_out,
    short_pooled,
    short_packed_out,
    short_packed_in,
    staged,
    pooled,
    packed_out,
    packed_in,
    table_out,
    table_in,
    table,
    order_out,
    order_in,
    enter_sem,
    in_send,
    in_recv,
    factor_sem,
    legendre_sem,
    table_send,
    table_recv,
    table_sem,
    stage_send,
    pool_recv,
    pack_send,
    pack_recv,
    relay_send,
    short_send,
    short_pool_recv,
    short_pack_send,
    short_pack_recv,
    spread_send,
    long_send,
    long_recv,
    out_send,
    out_recv,
    out_local,
    far_local,
):
    my_rad = lax.axis_index("rad")
    my_mode = lax.axis_index("mode")
    devices = rads * modes
    slots = entering.shape[0]
    parts = arrived.shape[0]
    packed = arrived.shape[3]
    radii = right_ref.shape[1]
    rows, columns = held.shape[1], held.shape[3]
    half = rads // 2
    across = rads // PLANES
    group_count = half * modes
    window_units = staged.shape[1]
    window_blocks = window_units * UNIT // BLOCK
    window = window_units * UNIT
    shares = short_out.shape[1]
    share_parts = parts // shares
    width = staged.shape[3]
    me = my_rad * modes + my_mode
    side = my_rad // half
    near_base = side * half
    far_base = half - near_base
    gate_base = half - across + side * across
    far_gate_base = half - side * across
    outer_base = side * (rads - across)
    place = lax.rem(my_rad, across)
    plane_base = my_rad - place
    is_gate = plane_base == gate_base
    my_group = (my_rad - near_base) * modes + my_mode

    def remote(source, target, send_sem, recv_sem, rad, mode):
        return pltpu.make_async_remote_copy(
            src_ref=source,
            dst_ref=target,
            send_sem=send_sem,
            recv_sem=recv_sem,
            device_id=(rad, mode),
            device_id_type=MESH,
        )

    def enter(c):
        slot = lax.rem(c, slots)
        return pltpu.make_async_copy(x_ref.at[c], entering.at[slot], enter_sem.at[slot])

    for c in range(min(slots, parts)):
        enter(c).start()
    fetches = (
        pltpu.make_async_copy(left_hbm, left_ref, factor_sem.at[0]),
        pltpu.make_async_copy(right_hbm, right_ref, factor_sem.at[1]),
    )
    fetch_legendre = pltpu.make_async_copy(legendre_ref, polynomial_rows, legendre_sem)
    fetch_legendre.start()
    for fetch in fetches:
        fetch.start()
    barrier = pltpu.get_barrier_semaphore()
    for ka in range(rads):
        for kb in range(modes):
            if ka or kb:
                peer = (lax.rem(my_rad + ka, rads), lax.rem(my_mode + kb, modes))
                pl.semaphore_signal(barrier, inc=1, device_id=peer, device_id_type=MESH)

    blocks = [DEGREES // BLOCK - order_ref[0, 0, s] // BLOCK for s in range(2)]
    short = jnp.where(blocks[0] <= blocks[1], 0, 1)
    short_blocks = jnp.minimum(jnp.minimum(blocks[0], blocks[1]), window_blocks)
    short_order = jnp.where(short == 0, order_ref[0, 0, 0], order_ref[0, 0, 1])
    unused = (short_order - BLOCK * (short_order // BLOCK)) // UNIT
    short_units = short_blocks * (BLOCK // UNIT) - unused
    lane = lax.broadcasted_iota(jnp.int32, table_out.shape, 1)
    entries = jnp.where(lane == 2, short_units, 0)
    entries = jnp.where(lane == 1, short, entries)
    table_out[...] = jnp.where(lane == 0, short_blocks, entries)

    def extent(device):
        count = table[device, 0, 0]
        short_first = table[device, 0, 1] == 0
        units = table[device, 0, 2]
        first = jnp.where(short_first, 0, window_blocks - count)
        first_unit = jnp.where(short_first, count * (BLOCK // UNIT) - units, window_units - units)
        return count, first, units, first_unit

    def turn(c):
        enter(c).wait()
        outgoing[c] = jnp.swapaxes(entering[lax.rem(c, slots)], 0, 1)

        @pl.when(c + slots < parts)
        def _():
            enter(c + slots).start()

    turn(0)
    pl.semaphore_wait(barrier, devices - 1)

    def send_part(c, carry):
        @pl.when(c > 0)
        def _():
            turn(c)

        for k in range(half):
            a = far_base + lax.rem(my_rad + k, half)
            remote(
                outgoing.at[c, a], arrived.at[c, my_rad], in_send, in_recv.at[c], a, my_mode
            ).start()
        for k in range(1, half):
            a = near_base + lax.rem(my_rad + k, half)
            remote(
                outgoing.at[c, a], arrived.at[c, my_rad], in_send, in_recv.at[c], a, my_mode
            ).start()
        pltpu.make_async_copy(outgoing.at[c, my_rad], arrived.at[c, my_rad], in_recv.at[c]).start()
        return carry

    lax.fori_loop(0, 1, send_part, 0)
    for k in range(1, devices):
        d = lax.rem(me + k, devices)
        remote(
            table_out,
            table_in.at[me],
            table_send,
            table_recv,
            d // modes,
            lax.rem(d, modes),
        ).start()
    pltpu.make_async_copy(table_out, table_in.at[me], table_recv).start()

    lax.fori_loop(1, EARLY, send_part, 0)

    fetch_legendre.wait()
    for b in range(modes):
        for y in range(across):
            lats = slice(b * columns + y * width, b * columns + (y + 1) * width)
            leading = polynomial_rows[:window, lats]
            trailing = polynomial_rows[packed - window :, lats]
            chosen = jnp.where(short == 0, leading, trailing)
            staged[b * across + y] = chosen.reshape(window_units, UNIT, width)
    for kb in range(modes):
        b = lax.rem(my_mode + kb, modes)
        for ky in range(across):
            y = lax.rem(place + ky, across)
            source = staged.at[b * across + y]
            target = pooled.at[my_group]
            if kb or ky:
                remote(source, target, stage_send, pool_recv, gate_base + y, b).start()
            else:

                @pl.when(is_gate)
                def _():
                    pltpu.make_async_copy(source, target, pool_recv).start()

                @pl.when(jnp.logical_not(is_gate))
                def _():
                    remote(source, target, stage_send, pool_recv, gate_base + y, b).start()

    lax.fori_loop(EARLY, parts, send_part, 0)

    position = lax.broadcasted_iota(jnp.int32, (1, packed), 1)
    live = []
    degree = jnp.zeros((1, packed), jnp.int32)
    for s in range(2):
        order = order_ref[0, 0, s]
        start = start_ref[0, 0, s]
        first_degree = BLOCK * (order // BLOCK)
        inside = (position >= start) & (position < start + DEGREES - first_degree)
        row_degree = first_degree + position - start
        degree = degree + jnp.where(inside, row_degree, 0)
        live.append(jnp.where(inside & (row_degree >= order), 1.0, 0.0).astype(jnp.float32))
    degree_level = degree.astype(jnp.float32)
    harmonic = degree_level * (degree_level + 1.0) / (DEGREES * DEGREES)
    covered = jnp.maximum(live[0], live[1])
    live_short = jnp.where(short == 0, live[0], live[1])
    live_long = jnp.where(short == 0, live[1], live[0])
    half_radii = half * rows
    row = lax.broadcasted_iota(jnp.int32, (2 * half_radii, half_radii), 0)
    column = lax.broadcasted_iota(jnp.int32, (2 * half_radii, half_radii), 1)
    doubling = jnp.where(row // 2 == column, 1.0, 0.0).astype(jnp.bfloat16)
    stretch = packed // 3 if packed % (3 * BLOCK) == 0 else packed
    parity = lax.broadcasted_iota(jnp.int32, (2 * half_radii, stretch), 0) % 2
    for fetch in fetches:
        fetch.wait()

    def send_long(c):
        for kb in range(modes):
            b = lax.rem(my_mode + kb, modes)
            for k in range(half):
                i = lax.rem(my_rad + k, half)
                remote(
                    long_out.at[c, b, i],
                    long_in.at[c, my_group],
                    long_send,
                    long_recv.at[c, my_rad - near_base],
                    far_base + i,
                    b,
                ).start()

    def one_part(c, carry):
        field = c // parts_count
        pltpu.make_async_copy(arrived.at[c], arrived.at[c], in_recv.at[c]).wait()
        rates = eigen_ref[pl.ds(field, 1), :]
        rates = jnp.transpose(jnp.broadcast_to(rates, (128, radii)))[:, 0:1]
        left = pieces_of(left_ref[field], 3)
        right = pieces_of(right_ref[field], 2)
        for first in range(0, packed, stretch):
            cut = slice(first, first + stretch)
            shrink = 1.0 + rates + diffusivity_ref[field] * harmonic[:, cut]
            values = arrived[c, :, :, cut].reshape(radii, stretch)
            turned = product(left[2], values) + product(left[1], values) + product(left[0], values)
            high, low = pieces_of(turned * (covered[:, cut] / shrink), 2)
            result = product(right[0], low) + product(right[1], high) + product(right[0], high)
            arrived[c, :, :, cut] = result.astype(jnp.bfloat16).reshape(rads, rows, stretch)

        far = arrived[c, pl.ds(far_base, half)].reshape(half_radii, packed).astype(jnp.float32)
        masked = (far * live_short).astype(jnp.bfloat16)
        masked = jnp.where(short == 0, masked[:, :window], masked[:, packed - window :])
        share, place_in_share = c // share_parts, lax.rem(c, share_parts)
        for i in range(half):
            for w in range(window_blocks):
                short_out[i, share, w, place_in_share] = masked[
                    i * rows : (i + 1) * rows, w * BLOCK : (w + 1) * BLOCK
                ]

        @pl.when(place_in_share == share_parts - 1)
        def _():
            for k in range(half):
                i = lax.rem(my_rad + k, half)
                y = lax.rem(i, across)
                b = i // across * shares + share
                source, target = short_out.at[i, share], short_pooled.at[my_group]
                local = is_gate & (y == place) & (b == my_mode)

                @pl.when(local)
                def _():
                    pltpu.make_async_copy(source, target, short_pool_recv).start()

                @pl.when(jnp.logical_not(local))
                def _():
                    remote(source, target, short_send, short_pool_recv, gate_base + y, b).start()

        @pl.when(c < EARLY)
        def _():
            far_part(c)

        @pl.when(is_gate)
        def _():
            near_part(c)

        @pl.when(c == EARLY - 1)
        def _():
            gather()

        return carry

    def far_part(c):
        far = arrived[c, pl.ds(far_base, half)].reshape(half_radii, packed).astype(jnp.float32)
        updated_far[...] = (far * live_long).astype(jnp.bfloat16)

        def far_mode(b, carry):
            lats = pl.ds(pl.multiple_of(b * columns, columns), columns)
            summed = product(updated_far[...], polynomial_rows[:, lats])
            long_out[c, b] = summed.astype(jnp.bfloat16).reshape(half, rows, columns)
            return carry

        lax.fori_loop(0, modes, far_mode, 0)
        send_long(c)

    def near_part(c):
        for first in range(0, packed, stretch):
            cut = slice(first, first + stretch)
            near = arrived[c, pl.ds(near_base, half), :, cut]
            doubled = product(doubling, near.reshape(half_radii, stretch))
            chosen = jnp.where(parity == 0, live[0][:, cut], live[1][:, cut])
            updated[:, cut] = (doubled * chosen).astype(jnp.bfloat16)

        def near_mode(kb, carry):
            b = lax.rem(my_mode + kb, modes)
            lats = pl.ds(pl.multiple_of(b * columns, columns), columns)
            summed = product(updated[...], polynomial_rows[:, lats])
            block = (c * modes + kb) * half
            held[pl.ds(block, half)] = summed.reshape(half, rows, 2, columns).astype(jnp.bfloat16)
            target = o_ref.at[c * devices + me]
            for k in range(1, half):
                i = lax.rem(my_rad + k, half)
                remote(held.at[block + i], target, out_send, out_recv, near_base + i, b).start()
            source = held.at[block + my_rad - near_base]

            @pl.when(kb > 0)
            def _():
                remote(source, target, out_send, out_recv, my_rad, b).start()

            @pl.when(kb == 0)
            def _():
                pltpu.make_async_copy(source, target, out_local).start()

            return carry

        lax.fori_loop(0, modes, near_mode, 0)

    piece = unit_room // PIECES
    short_piece = block_room // PIECES
    ahead = (packed_in.shape[1] - unit_room) // 2

    def gather():
        pltpu.make_async_copy(table_in, table_in, table_recv).wait()
        to_scalars = pltpu.make_async_copy(table_in, table, table_sem)
        to_scalars.start()
        to_scalars.wait()

        @pl.when(is_gate)
        def _():
            shape = order_out.shape[1:]
            index = BLOCK * lax.broadcasted_iota(jnp.int32, shape, 0) + lax.broadcasted_iota(
                jnp.int32, shape, 1
            )
            unit_source = jnp.zeros(shape, jnp.int32)
            block_source = jnp.zeros(shape, jnp.int32)
            unit_offset, block_offset = jnp.int32(0), jnp.int32(0)
            for group in range(group_count):
                count, first, units, first_unit = extent(near_base * modes + group)
                inside = (index >= unit_offset) & (index < unit_offset + units)
                shift = group * window_units + first_unit - unit_offset
                unit_source = jnp.where(inside, index + shift, unit_source)
                inside = (index >= block_offset) & (index < block_offset + count)
                shift = group * window_blocks + first - block_offset
                block_source = jnp.where(inside, index + shift, block_source)
                unit_offset = unit_offset + units
                block_offset = block_offset + count
            order_out[0] = unit_source
            order_out[1] = block_source
            to_scalars = pltpu.make_async_copy(order_out, order_in, table_sem)
            to_scalars.start()
            pltpu.make_async_copy(pooled, pooled, pool_recv).wait()
            to_scalars.wait()

            def one_unit(j, carry):
                source = order_in[0, j // BLOCK, lax.rem(j, BLOCK)]
                group = jnp.clip(source // window_units, 0, group_count - 1)
                unit = jnp.clip(source - group * window_units, 0, window_units - 1)
                packed_out[j] = pooled[group, unit]
                return carry

            def pack(p, carry):
                lax.fori_loop(p * piece, (p + 1) * piece, one_unit, 0)
                remote(
                    packed_out.at[pl.ds(p * piece, piece)],
                    packed_in.at[place, pl.ds(ahead + p * piece, piece)],
                    pack_send,
                    pack_recv.at[place, p],
                    far_gate_base + place,
                    my_mode,
                ).start()
                return carry

            lax.fori_loop(0, PIECES, pack, 0)

    def gather_short():
        pltpu.make_async_copy(short_pooled, short_pooled, short_pool_recv).wait()

        def one_block(j, carry):
            source = order_in[1, j // BLOCK, lax.rem(j, BLOCK)]
            group = jnp.clip(source // window_blocks, 0, group_count - 1)
            block = jnp.clip(source - group * window_blocks, 0, window_blocks - 1)
            short_packed_out[j] = short_pooled[group, block]
            return carry

        def pack(p, carry):
            lax.fori_loop(p * short_piece, (p + 1) * short_piece, one_block, 0)
            some = pl.ds(p * short_piece, short_piece)
            remote(
                short_packed_out.at[some],
                short_packed_in.at[lax.rem(my_mode, shares), some],
                short_pack_send,
                short_pack_recv.at[lax.rem(my_mode, shares), p],
                far_base + my_mode // shares * across + place,
                my_mode,
            ).start()
            return carry

        lax.fori_loop(0, PIECES, pack, 0)

    blank = jnp.zeros((ahead, UNIT, width), jnp.bfloat16)
    for y in range(across):
        packed_in[y, :ahead] = blank
        packed_in[y, ahead + unit_room :] = blank

    lax.fori_loop(0, parts, one_part, 0)

    def arrived_piece(y, p):
        some = packed_in.at[y, pl.ds(ahead + p * piece, piece)]
        return pltpu.make_async_copy(some, some, pack_recv.at[y, p])

    def relay(p, carry):
        arrived_piece(place, p).wait()
        some = packed_in.at[place, pl.ds(ahead + p * piece, piece)]

        @pl.when(is_gate)
        def _():
            remote(
                some, some, relay_send, pack_recv.at[place, p], outer_base + place, my_mode
            ).start()

        for k in range(1, across):
            remote(
                some,
                some,
                relay_send,
                pack_recv.at[place, p],
                plane_base + lax.rem(place + k, across),
                my_mode,
            ).start()
        return carry

    def short_piece_of(share, p):
        some = short_packed_in.at[share, pl.ds(p * short_piece, short_piece)]
        return pltpu.make_async_copy(some, some, short_pack_recv.at[share, p])

    my_share = lax.rem(my_mode, shares)
    is_spreader = my_mode // shares == (my_rad - near_base) // across

    def spread(p, carry):
        short_piece_of(my_share, p).wait()
        some = short_packed_in.at[my_share, pl.ds(p * short_piece, short_piece)]
        arrival = short_pack_recv.at[my_share, p]

        @pl.when(is_spreader)
        def _():
            for k in range(shares, modes, shares):
                mate = lax.rem(my_mode + k, modes)
                remote(some, some, spread_send, arrival, my_rad, mate).start()

        for k in range(1, shares):
            sibling = my_mode - my_share + lax.rem(my_share + k, shares)
            remote(some, some, spread_send, arrival, my_rad, sibling).start()
        return carry

    def late_part(c, carry):
        @pl.when(c >= EARLY)
        def _():
            far_part(c)

        @pl.when(jnp.logical_not(is_gate))
        def _():
            near_part(c)

        @pl.when((c == SHORT_AFTER) & is_gate)
        def _():
            lax.fori_loop(0, PIECES // 2, relay, 0)
            gather_short()
            lax.fori_loop(PIECES // 2, PIECES, relay, 0)

        return carry

    lax.fori_loop(0, parts, late_part, 0)

    @pl.when(jnp.logical_not(is_gate))
    def _():
        lax.fori_loop(0, PIECES, relay, 0)

    lax.fori_loop(0, PIECES, spread, 0)

    other_blocks = held.at[pl.ds(0, parts * (group_count - 1))]
    pltpu.make_async_copy(other_blocks, other_blocks, out_send).wait()
    own = pl.ds(0, parts)
    pltpu.make_async_copy(held.at[own], o_ref.at[own], out_local).wait()

    def arrived_pieces(p, carry):
        for k in range(1, across):
            arrived_piece(lax.rem(place + k, across), p).wait()
        return carry

    lax.fori_loop(0, PIECES, arrived_pieces, 0)

    def arrived_shorts(p, carry):
        for k in range(1, shares):
            short_piece_of(lax.rem(my_mode + k, shares), p).wait()

        return carry

    lax.fori_loop(0, PIECES, arrived_shorts, 0)

    sent_parts = outgoing.at[:, pl.ds(0, rads - 1)]

    pltpu.make_async_copy(sent_parts, sent_parts, in_send).wait()
    counts = [table[far_base * modes + group, 0, 0] for group in range(group_count)]
    units_of = [table[far_base * modes + group, 0, 2] for group in range(group_count)]

    def one_group(group, carry):
        count, first, _, first_unit = extent(far_base * modes + group)
        offset, unit_offset = jnp.int32(0), jnp.int32(0)
        for k in range(group_count - 1):
            offset = offset + jnp.where(k < group, counts[k], 0)
            unit_offset = unit_offset + jnp.where(k < group, units_of[k], 0)
        factors = []
        for share in range(shares):
            taken = []
            for w in range(window_blocks):
                j = jnp.clip(offset + w - first, 0, block_room - 1)
                block = short_packed_in[share, j].reshape(share_parts * rows, BLOCK)
                valid = (w >= first) & (w < first + count)
                taken.append(jnp.where(valid, block, jnp.zeros_like(block)))
            factors.append(jnp.concatenate(taken, axis=1))
        factors = jnp.concatenate(factors, axis=0)
        begin = jnp.clip(ahead + unit_offset - first_unit, 0, ahead + unit_room)
        for y in range(across):
            taken = [packed_in[y, begin + k] for k in range(window_units)]
            summed = product(factors, jnp.concatenate(taken, axis=0))
            lats = pl.ds(
                pl.multiple_of((group // rads) * columns + y * width, width), width
            )
            outgoing[:, lax.rem(group, rads), :, lats] = summed.reshape(parts, rows, width).astype(
                jnp.bfloat16
            )
        return carry

    lax.fori_loop(0, group_count, one_group, 0)

    together = modes
    size = 2 * together * rows
    row = lax.broadcasted_iota(jnp.int32, (size, size), 0)
    column = lax.broadcasted_iota(jnp.int32, (size, size), 1)
    origin = (row % 2) * (together * rows) + (row // (2 * rows)) * rows + (row % (2 * rows)) // 2
    merging = jnp.where(column == origin, 1.0, 0.0).astype(jnp.bfloat16)

    def merge_part(c, carry):
        def merge_some(q, carry):
            row_groups = long_in.at[c, pl.ds(q * together, together)]
            pltpu.make_async_copy(row_groups, row_groups, long_recv.at[c, q]).wait()
            for y in range(across):
                lats = slice(y * width, (y + 1) * width)
                leading, trailing = [], []
                for k in range(together):
                    group = q * together + k
                    taken = pl.ds(
                        pl.multiple_of((group // rads) * columns + y * width, width), width
                    )
                    from_short = outgoing[c, lax.rem(group, rads), :, taken]
                    from_long = long_in[c, group, :, lats]
                    short_first = table[far_base * modes + group, 0, 1] == 0
                    leading.append(jnp.where(short_first, from_short, from_long))
                    trailing.append(jnp.where(short_first, from_long, from_short))
                merged = product(merging, jnp.concatenate(leading + trailing, axis=0))
                block = pl.ds(c * group_count + q * together, together)
                held[block, :, :, lats] = merged.reshape(together, rows, 2, width).astype(
                    jnp.bfloat16
                )
            pltpu.make_async_copy(
                held.at[pl.ds(c * group_count + q * together, together)],
                o_ref.at[pl.ds(c * devices + far_base * modes + q * together, together)],
                far_local,
            ).start()
            return carry

        lax.fori_loop(0, group_count // together, merge_some, 0)
        return carry

    lax.fori_loop(0, parts, merge_part, 0)

    overfull = jnp.int32(0)
    for begin in (0, group_count):
        blocks_used, units_used = jnp.int32(0), jnp.int32(0)
        for group in range(begin, begin + group_count):
            blocks_used = blocks_used + table[group, 0, 0]
            units_used = units_used + table[group, 0, 2]
        overfull = jnp.where((blocks_used > block_room) | (units_used > unit_room), 1, overfull)
    flag_ref[0, 0] = overfull

    sent = table_in.at[pl.ds(0, devices - 1)]
    pltpu.make_async_copy(sent, sent, table_send).wait()
    sent = staged.at[pl.ds(0, modes * across - 1)]
    pltpu.make_async_copy(sent, sent, stage_send).wait()
    for share in range(shares):
        for i in range(half):
            sent = short_out.at[i, share]
            local = is_gate & (i % across == place) & (i // across * shares + share == my_mode)

            @pl.when(jnp.logical_not(local))
            def _():
                pltpu.make_async_copy(sent, sent, short_send).wait()

    for k in range(1, shares):
        pltpu.make_async_copy(short_packed_out, short_packed_out, spread_send).wait()

    @pl.when(is_spreader)
    def _():
        for k in range(shares, modes, shares):
            pltpu.make_async_copy(short_packed_out, short_packed_out, spread_send).wait()

    pltpu.make_async_copy(long_out, long_out, long_send).wait()

    @pl.when(is_gate)
    def _():
        pltpu.make_async_copy(packed_out, packed_out, pack_send).wait()
        pltpu.make_async_copy(packed_out, packed_out, relay_send).wait()
        pltpu.make_async_copy(short_packed_out, short_packed_out, short_pack_send).wait()

    @pl.when(jnp.logical_not(is_gate))
    def _():
        pltpu.make_async_copy(staged.at[0], staged.at[0], stage_send).wait()

    for k in range(1, across):
        pltpu.make_async_copy(packed_out, packed_out, relay_send).wait()
    remote_blocks = o_ref.at[pl.ds(0, parts * (group_count - 1))]
    pltpu.make_async_copy(remote_blocks, remote_blocks, out_recv).wait()
    far_blocks = pl.ds(0, parts * group_count)
    pltpu.make_async_copy(held.at[far_blocks], o_ref.at[far_blocks], far_local).wait()


def factored(rads, modes, unit_room, block_room, arguments):
    (
        coefficients,
        legendre,
        radial_left_factor,
        radial_right,
        eigen_rates,
        diffusivity,
        slot_order,
        slot_start,
    ) = arguments
    packed, lats = legendre.shape[2:]
    radii = radial_right.shape[1]
    fields, parts_count = coefficients.shape[:2]
    parts = fields * parts_count
    devices = rads * modes
    rows, columns = radii // rads, lats // modes
    half, across = rads // 2, rads // PLANES
    groups, width = half * modes, columns // across
    window = packed // BLOCK // 2 * BLOCK
    shares = 2 * modes // PLANES
    smem = pl.BlockSpec(memory_space=pltpu.SMEM)
    vmem = pl.BlockSpec(memory_space=pltpu.VMEM)
    hbm = pl.BlockSpec(memory_space=pltpu.HBM)
    kept = jnp.bfloat16
    dma = pltpu.SemaphoreType.DMA
    return pl.pallas_call(
        functools.partial(factored_kernel, rads, modes, parts_count, unit_room, block_room),
        out_shape=(
            pltpu.VMEM((parts * devices, rows, 2, columns), kept),
            jax.ShapeDtypeStruct((1, 1), jnp.int32),
        ),
        in_specs=[smem, smem, smem, vmem, hbm, hbm, hbm, hbm],
        out_specs=(pl.BlockSpec(memory_space=pl.ANY), smem),
        scratch_shapes=[
            pltpu.VMEM(radial_left_factor.shape, jnp.float32),
            pltpu.VMEM(radial_right.shape, jnp.float32),
            pltpu.VMEM((min(3, parts), rows, rads, packed), kept),
            pltpu.VMEM((parts, rads, rows, packed), kept),
            pltpu.VMEM((parts, rads, rows, packed), kept),
            pltpu.VMEM((packed, lats), kept),
            pltpu.VMEM((radii, packed), kept),
            pltpu.VMEM((radii // 2, packed), kept),
            pltpu.VMEM((parts * groups, rows, 2, columns), kept),
            pltpu.VMEM((parts, modes, half, rows, columns), kept),
            pltpu.VMEM((parts, groups, rows, columns), kept),
            pltpu.VMEM((half, shares, window // BLOCK, parts // shares, rows, BLOCK), kept),
            pltpu.VMEM((groups, window // BLOCK, parts // shares, rows, BLOCK), kept),
            pltpu.VMEM((block_room, parts // shares, rows, BLOCK), kept),
            pltpu.VMEM((shares, block_room, parts // shares, rows, BLOCK), kept),
            pltpu.VMEM((modes * across, window // UNIT, UNIT, width), kept),
            pltpu.VMEM((groups, window // UNIT, UNIT, width), kept),
            pltpu.VMEM((unit_room, UNIT, width), kept),
            pltpu.VMEM((across, unit_room + 2 * window // UNIT, UNIT, width), kept),
            pltpu.VMEM((8, 128), jnp.int32),
            pltpu.VMEM((devices, 8, 128), jnp.int32),
            pltpu.SMEM((devices, 8, 128), jnp.int32),
            pltpu.VMEM((2, 8, 128), jnp.int32),
            pltpu.SMEM((2, 8, 128), jnp.int32),
            dma((min(3, parts),)),
            dma,
            dma((parts,)),
            dma((2,)),
            dma,
            dma,
            dma,
            dma,
            dma,
            dma,
            dma,
            dma((across, PIECES)),
            dma,
            dma,
            dma,
            dma,
            dma((shares, PIECES)),
            dma,
            dma,
            dma((parts, half)),
            dma,
            dma,
            dma,
            dma,
        ],
        compiler_params=pltpu.CompilerParams(
            collective_id=1, has_side_effects=True, vmem_limit_bytes=50 * 2**20
        ),
    )(
        slot_order,
        slot_start,
        diffusivity,
        eigen_rates,
        radial_left_factor,
        radial_right,
        coefficients.reshape(parts, rows, rads, packed),
        legendre.reshape(packed, lats),
    )


def dense(
    rads,
    modes,
    arguments,
):
    (
        coefficients,
        legendre,
        radial_left_factor,
        radial_right,
        eigen_rates,
        diffusivity,
        slot_order,
        slot_start,
    ) = arguments
    packed, lats = legendre.shape[2:]
    radii = radial_right.shape[1]
    fields, parts_count = coefficients.shape[:2]
    parts = fields * parts_count
    devices = rads * modes
    rows, columns = radii // rads, lats // modes
    smem = pl.BlockSpec(memory_space=pltpu.SMEM)
    vmem = pl.BlockSpec(memory_space=pltpu.VMEM)
    hbm = pl.BlockSpec(memory_space=pltpu.HBM)
    return pl.pallas_call(
        functools.partial(whole_kernel, rads, modes, parts_count),
        out_shape=pltpu.VMEM((parts * devices, rows, 2, columns), jnp.bfloat16),
        in_specs=[smem, smem, smem, vmem, hbm, hbm, hbm, hbm],
        out_specs=pl.BlockSpec(memory_space=pl.ANY),
        scratch_shapes=[
            pltpu.VMEM(radial_left_factor.shape, jnp.float32),
            pltpu.VMEM(radial_right.shape, jnp.float32),
            pltpu.VMEM((parts, rows, rads, packed), jnp.bfloat16),
            pltpu.VMEM((parts, rads, rows, packed), jnp.bfloat16),
            pltpu.VMEM((parts, rads, rows, packed), jnp.bfloat16),
            pltpu.VMEM((packed, lats), jnp.bfloat16),
            pltpu.VMEM((2 * radii, packed), jnp.bfloat16),
            pltpu.VMEM((parts * devices, rows, 2, columns), jnp.bfloat16),
            pltpu.SemaphoreType.DMA((parts,)),
            pltpu.SemaphoreType.DMA,
            pltpu.SemaphoreType.DMA((parts,)),
            pltpu.SemaphoreType.DMA((2,)),
            pltpu.SemaphoreType.DMA,
            pltpu.SemaphoreType.DMA,
            pltpu.SemaphoreType.DMA,
            pltpu.SemaphoreType.DMA,
        ],
        compiler_params=pltpu.CompilerParams(
            collective_id=0, has_side_effects=True, vmem_limit_bytes=46 * 2**20
        ),
    )(
        slot_order,
        slot_start,
        diffusivity,
        eigen_rates,
        radial_left_factor,
        radial_right,
        coefficients.reshape(parts, rows, rads, packed),
        legendre.reshape(packed, lats),
    )


def on_device(rads, modes, *arguments):
    coefficients, legendre, _, radial_right = arguments[:4]
    packed, lats = legendre.shape[2:]
    rows, columns = radial_right.shape[1] // rads, lats // modes
    fields, parts_count = coefficients.shape[:2]
    parts = fields * parts_count
    half, across = rads // 2, rads // PLANES
    groups = half * modes
    window_blocks = packed // BLOCK // 2
    window_units = window_blocks * BLOCK // UNIT
    block_room = 3 * groups * window_blocks // 4
    unit_room = 21 * groups * window_units // 32
    shares = 2 * modes // PLANES
    fits = (
        rads % PLANES == 0
        and 2 * modes % PLANES == 0
        and parts % max(shares, 1) == 0
        and columns % (BLOCK * across) == 0
        and groups <= rads * (packed // columns)
        and unit_room % PIECES == 0
        and unit_room <= 8 * BLOCK
        and across * unit_room * UNIT * (columns // across) <= 2**22
    )
    if fits:
        landed, flag = factored(rads, modes, unit_room, block_room, arguments)
        landed = lax.switch(
            flag[0, 0], (lambda: landed, lambda: dense(rads, modes, arguments))
        )
    else:
        landed = dense(rads, modes, arguments)
    return landed.reshape(fields, parts_count, rads, modes, rows, 2, columns)


def solution(mesh):
    rads, modes = mesh.shape["rad"], mesh.shape["mode"]
    return jax.shard_map(
        functools.partial(on_device, rads, modes),
        mesh=mesh,
        in_specs=(
            P(None, None, "rad", None, "mode", None),
            P("rad", "mode", None, None),
            P(),
            P(),
            P(),
            P(),
            P("rad", "mode", None),
            P("rad", "mode", None),
        ),
        out_specs=P(None, None, None, None, "rad", None, "mode"),
        check_vma=False,
    )
```

profile of v0, /device:TPU:3, one launch (start us, length us, event | category | flops | bytes accessed | tf_op | source)
XLA Modules:
  0.0 319.5 jit_solution(12533562952756330934)
XLA Ops:
  0.0 313.9 %shard_map.84 = (bf16[192,32,2,512]{3,2,1,0:T(2,128)(2,1)S(1)}, s32[1,1]{1,0:T(1,128)}) custom-call(s32[1,1,2]{2,1,0:T(1,128)} %order_ref.1, s32[1,1,2]{2,1,0:T(1,128)} %start_ref.1, f32[3]{0:T(128)} %diffusivity_ref.1, f32[3,256]{1,0:T(4,128)} %eigen_ref.1, f32[3,256,256]{2,1,0:T(8,128)} %left_hbm.1, f32[3,256,256]{2,1,0:T(8,128)} %right_hbm.1, ...), custom_call_target="tpu_custom_call" | custom-call | tf_op jit(solution)/shard_map/pallas_call | solution.py:892
  314.5 0.2 conditional.1
  314.7 4.8 %copy.16 = bf16[3,2,8,4,32,2,512]{6,5,4,3,2,1,0:T(2,128)(2,1)} copy(bf16[3,2,8,4,32,2,512]{6,5,4,3,2,1,0:T(2,128)(2,1)S(1)} %get-tuple-element.39) | data formatting | bytes 25165824
where the time goes:
time: 321 us; the launch traced here: 319 us
  Pallas kernels  314 us (98%)
  local copies, waits for them, and re-layouts  4.78 us (1%)
    pallas_call x1, Pallas kernels, factored(): pl.pallas_call(functools.partial(factored_kernel, rads, modes, parts_coun...  314 us

commit v1 on v0

--- a/solution.py
+++ b/solution.py
@@ -203,16 +203,20 @@
     parts_count,
     unit_room,
     block_room,
-    order_ref,
-    start_ref,
-    diffusivity_ref,
-    eigen_ref,
+    order_hbm,
+    start_hbm,
+    diffusivity_hbm,
+    eigen_hbm,
     left_hbm,
     right_hbm,
     x_ref,
     legendre_ref,
     o_ref,
     flag_ref,
+    order_ref,
+    start_ref,
+    diffusivity_ref,
+    eigen_ref,
     left_ref,
     right_ref,
     entering,
@@ -261,6 +265,7 @@
     out_recv,
     out_local,
     far_local,
+    setting_sem,
 ):
     my_rad = lax.axis_index("rad")
     my_mode = lax.axis_index("mode")
@@ -301,11 +306,27 @@
             device_id_type=MESH,
         )
 
+    barrier = pltpu.get_barrier_semaphore()
+    for ka in range(rads):
+        for kb in range(modes):
+            if ka or kb:
+                peer = (lax.rem(my_rad + ka, rads), lax.rem(my_mode + kb, modes))
+                pl.semaphore_signal(barrier, inc=1, device_id=peer, device_id_type=MESH)
+
     def enter(c):
         slot = lax.rem(c, slots)
         return pltpu.make_async_copy(x_ref.at[c], entering.at[slot], enter_sem.at[slot])
 
-    for c in range(min(slots, parts)):
+    settings = (
+        pltpu.make_async_copy(order_hbm, order_ref, setting_sem.at[0]),
+        pltpu.make_async_copy(start_hbm, start_ref, setting_sem.at[1]),
+        pltpu.make_async_copy(diffusivity_hbm, diffusivity_ref, setting_sem.at[2]),
+        pltpu.make_async_copy(eigen_hbm, eigen_ref, setting_sem.at[3]),
+    )
+    enter(0).start()
+    for setting in settings:
+        setting.start()
+    for c in range(1, min(slots, parts)):
         enter(c).start()
     fetches = (
         pltpu.make_async_copy(left_hbm, left_ref, factor_sem.at[0]),
@@ -315,12 +336,25 @@
     fetch_legendre.start()
     for fetch in fetches:
         fetch.start()
-    barrier = pltpu.get_barrier_semaphore()
-    for ka in range(rads):
-        for kb in range(modes):
-            if ka or kb:
-                peer = (lax.rem(my_rad + ka, rads), lax.rem(my_mode + kb, modes))
-                pl.semaphore_signal(barrier, inc=1, device_id=peer, device_id_type=MESH)
+
+    def extent(device):
+        count = table[device, 0, 0]
+        short_first = table[device, 0, 1] == 0
+        units = table[device, 0, 2]
+        first = jnp.where(short_first, 0, window_blocks - count)
+        first_unit = jnp.where(short_first, count * (BLOCK // UNIT) - units, window_units - units)
+        return count, first, units, first_unit
+
+    def turn(c):
+        enter(c).wait()
+        outgoing[c] = jnp.swapaxes(entering[lax.rem(c, slots)], 0, 1)
+
+        @pl.when(c + slots < parts)
+        def _():
+            enter(c + slots).start()
+
+    turn(0)
+    settings[0].wait()
 
     blocks = [DEGREES // BLOCK - order_ref[0, 0, s] // BLOCK for s in range(2)]
     short = jnp.where(blocks[0] <= blocks[1], 0, 1)
@@ -333,23 +367,6 @@
     entries = jnp.where(lane == 1, short, entries)
     table_out[...] = jnp.where(lane == 0, short_blocks, entries)
 
-    def extent(device):
-        count = table[device, 0, 0]
-        short_first = table[device, 0, 1] == 0
-        units = table[device, 0, 2]
-        first = jnp.where(short_first, 0, window_blocks - count)
-        first_unit = jnp.where(short_first, count * (BLOCK // UNIT) - units, window_units - units)
-        return count, first, units, first_unit
-
-    def turn(c):
-        enter(c).wait()
-        outgoing[c] = jnp.swapaxes(entering[lax.rem(c, slots)], 0, 1)
-
-        @pl.when(c + slots < parts)
-        def _():
-            enter(c + slots).start()
-
-    turn(0)
     pl.semaphore_wait(barrier, devices - 1)
 
     def send_part(c, carry):
@@ -413,6 +430,8 @@
 
     lax.fori_loop(EARLY, parts, send_part, 0)
 
+    for setting in settings[1:]:
+        setting.wait()
     position = lax.broadcasted_iota(jnp.int32, (1, packed), 1)
     live = []
     degree = jnp.zeros((1, packed), jnp.int32)
@@ -885,7 +904,6 @@
     window = packed // BLOCK // 2 * BLOCK
     shares = 2 * modes // PLANES
     smem = pl.BlockSpec(memory_space=pltpu.SMEM)
-    vmem = pl.BlockSpec(memory_space=pltpu.VMEM)
     hbm = pl.BlockSpec(memory_space=pltpu.HBM)
     kept = jnp.bfloat16
     dma = pltpu.SemaphoreType.DMA
@@ -895,9 +913,13 @@
             pltpu.VMEM((parts * devices, rows, 2, columns), kept),
             jax.ShapeDtypeStruct((1, 1), jnp.int32),
         ),
-        in_specs=[smem, smem, smem, vmem, hbm, hbm, hbm, hbm],
+        in_specs=[hbm] * 8,
         out_specs=(pl.BlockSpec(memory_space=pl.ANY), smem),
         scratch_shapes=[
+            pltpu.SMEM(slot_order.shape, jnp.int32),
+            pltpu.SMEM(slot_start.shape, jnp.int32),
+            pltpu.SMEM(diffusivity.shape, jnp.float32),
+            pltpu.VMEM(eigen_rates.shape, jnp.float32),
             pltpu.VMEM(radial_left_factor.shape, jnp.float32),
             pltpu.VMEM(radial_right.shape, jnp.float32),
             pltpu.VMEM((min(3, parts), rows, rads, packed), kept),
@@ -946,6 +968,7 @@
             dma,
             dma,
             dma,
+            dma((4,)),
         ],
         compiler_params=pltpu.CompilerParams(
             collective_id=1, has_side_effects=True, vmem_limit_bytes=50 * 2**20

time: 321 us -> 320 us (level)
  no operation moved by 1% of the time
where the time goes in v1:
time: 320 us; the launch traced here: 318 us
  Pallas kernels  313 us (98%)
  local copies, waits for them, and re-layouts  4.78 us (1%)
    pallas_call x1, Pallas kernels, factored(): pl.pallas_call(functools.partial(factored_kernel, rads, modes, parts_coun...  313 us

profile of v1, /device:TPU:3, one launch (start us, length us, event | category | flops | bytes accessed | tf_op | source)
XLA Modules:
  0.0 318.5 jit_solution(262093155807242191)
XLA Ops:
  0.0 312.9 %shard_map.84 = (bf16[192,32,2,512]{3,2,1,0:T(2,128)(2,1)S(1)}, s32[1,1]{1,0:T(1,128)}) custom-call(s32[1,1,2]{2,1,0:T(1,128)} %order_hbm.1, s32[1,1,2]{2,1,0:T(1,128)} %start_hbm.1, f32[3]{0:T(128)} %diffusivity_hbm.1, f32[3,256]{1,0:T(4,128)} %eigen_hbm.1, f32[3,256,256]{2,1,0:T(8,128)} %left_hbm.1, f32[3,256,256]{2,1,0:T(8,128)} %right_hbm.1, ...), custom_call_target="tpu_custom_call" | custom-call | tf_op jit(solution)/shard_map/pallas_call | solution.py:910
  313.5 0.2 conditional.1
  313.7 4.8 %copy.16 = bf16[3,2,8,4,32,2,512]{6,5,4,3,2,1,0:T(2,128)(2,1)} copy(bf16[3,2,8,4,32,2,512]{6,5,4,3,2,1,0:T(2,128)(2,1)S(1)} %get-tuple-element.39) | data formatting | bytes 25165824

commit v2 on v1

--- a/solution.py
+++ b/solution.py
@@ -264,7 +264,6 @@
     out_send,
     out_recv,
     out_local,
-    far_local,
     setting_sem,
 ):
     my_rad = lax.axis_index("rad")
@@ -307,8 +306,8 @@
         )
 
     barrier = pltpu.get_barrier_semaphore()
-    for ka in range(rads):
-        for kb in range(modes):
+    for ka in far_first(rads):
+        for kb in far_first(modes):
             if ka or kb:
                 peer = (lax.rem(my_rad + ka, rads), lax.rem(my_mode + kb, modes))
                 pl.semaphore_signal(barrier, inc=1, device_id=peer, device_id_type=MESH)
@@ -816,21 +815,16 @@
                     leading.append(jnp.where(short_first, from_short, from_long))
                     trailing.append(jnp.where(short_first, from_long, from_short))
                 merged = product(merging, jnp.concatenate(leading + trailing, axis=0))
-                block = pl.ds(c * group_count + q * together, together)
-                held[block, :, :, lats] = merged.reshape(together, rows, 2, width).astype(
+                block = pl.ds(c * devices + far_base * modes + q * together, together)
+                o_ref[block, :, :, lats] = merged.reshape(together, rows, 2, width).astype(
                     jnp.bfloat16
                 )
-            pltpu.make_async_copy(
-                held.at[pl.ds(c * group_count + q * together, together)],
-                o_ref.at[pl.ds(c * devices + far_base * modes + q * together, together)],
-                far_local,
-            ).start()
             return carry
 
         lax.fori_loop(0, group_count // together, merge_some, 0)
         return carry
 
-    lax.fori_loop(0, parts, merge_part, 0)
+    lax.fori_loop(0, parts - 1, merge_part, 0)
 
     overfull = jnp.int32(0)
     for begin in (0, group_count):
@@ -862,7 +856,6 @@
         for k in range(shares, modes, shares):
             pltpu.make_async_copy(short_packed_out, short_packed_out, spread_send).wait()
 
-    pltpu.make_async_copy(long_out, long_out, long_send).wait()
 
     @pl.when(is_gate)
     def _():
@@ -878,8 +871,9 @@
         pltpu.make_async_copy(packed_out, packed_out, relay_send).wait()
     remote_blocks = o_ref.at[pl.ds(0, parts * (group_count - 1))]
     pltpu.make_async_copy(remote_blocks, remote_blocks, out_recv).wait()
-    far_blocks = pl.ds(0, parts * group_count)
-    pltpu.make_async_copy(held.at[far_blocks], o_ref.at[far_blocks], far_local).wait()
+
+    lax.fori_loop(parts - 1, parts, merge_part, 0)
+    pltpu.make_async_copy(long_out, long_out, long_send).wait()
 
 
 def factored(rads, modes, unit_room, block_room, arguments):
@@ -914,7 +908,7 @@
             jax.ShapeDtypeStruct((1, 1), jnp.int32),
         ),
         in_specs=[hbm] * 8,
-        out_specs=(pl.BlockSpec(memory_space=pl.ANY), smem),
+        out_specs=(pl.BlockSpec(memory_space=pltpu.VMEM), smem),
         scratch_shapes=[
             pltpu.SMEM(slot_order.shape, jnp.int32),
             pltpu.SMEM(slot_start.shape, jnp.int32),
@@ -964,7 +958,6 @@
             dma,
             dma,
             dma((parts, half)),
-            dma,
             dma,
             dma,
             dma,

time: 320 us -> 319 us (level)
  no operation moved by 1% of the time
where the time goes in v2:
time: 319 us; the launch traced here: 318 us
  Pallas kernels  312 us (98%)
  local copies, waits for them, and re-layouts  4.78 us (1%)
    pallas_call x1, Pallas kernels, factored(): pl.pallas_call(functools.partial(factored_kernel, rads, modes, parts_coun...  312 us

profile of v2, /device:TPU:3, one launch (start us, length us, event | category | flops | bytes accessed | tf_op | source)
XLA Modules:
  0.0 318.0 jit_solution(12139204178500146251)
XLA Ops:
  0.0 312.4 %shard_map.84 = (bf16[192,32,2,512]{3,2,1,0:T(2,128)(2,1)S(1)}, s32[1,1]{1,0:T(1,128)}) custom-call(s32[1,1,2]{2,1,0:T(1,128)} %order_hbm.1, s32[1,1,2]{2,1,0:T(1,128)} %start_hbm.1, f32[3]{0:T(128)} %diffusivity_hbm.1, f32[3,256]{1,0:T(4,128)} %eigen_hbm.1, f32[3,256,256]{2,1,0:T(8,128)} %left_hbm.1, f32[3,256,256]{2,1,0:T(8,128)} %right_hbm.1, ...), custom_call_target="tpu_custom_call" | custom-call | tf_op jit(solution)/shard_map/pallas_call | solution.py:904
  313.0 0.2 conditional.1
  313.2 4.8 %copy.16 = bf16[3,2,8,4,32,2,512]{6,5,4,3,2,1,0:T(2,128)(2,1)} copy(bf16[3,2,8,4,32,2,512]{6,5,4,3,2,1,0:T(2,128)(2,1)S(1)} %get-tuple-element.39) | data formatting | bytes 25165824
